TPU v7x, 32 devices: a whole 2x2x4 slice. The times are simulated.
32 devices in a mesh: tm: 2 (over y), space: 16 (over z, x, core).
Axes of the slice: x: 2, y: 2, z: 4, core: 2. Of those that a mesh axis runs over, the one named last changes fastest.
Arguments:
- noisy_state: float32 [8, 2, 256, 256], P('tm', None, 'space'), may hold values from -6 to 6
- fresh_noise: float32 [8, 2, 256, 256], P('tm', None, 'space'), may hold values from -6 to 6
- level_index: int32 [1], replicated, may hold values from 1 to 31
- station_obs: float32 [8, 2, 2048], P('tm', None, 'space'), may hold values from -6 to 6
- obs_variance: float32 [2048], P('space'), may hold values from 0.05 to 0.5
- station_owner: int32 [2048, 1], P('space'), may hold values from 0 to 15; in each aligned block of 128 rows (0 to 127, 128 to 255, ...) at most 32 rows name the same one
- station_cell: int32 [2048], P('space'), may hold values from 0 to 4095
- conv_in: bfloat16 [3, 64, 48], replicated, may hold values from -0.5 to 0.5
- conv_mid: bfloat16 [3, 64, 192], replicated, may hold values from -0.25 to 0.25
- conv_res: bfloat16 [3, 64, 192], replicated, may hold values from -0.25 to 0.25
- conv_out: bfloat16 [3, 16, 192], replicated, may hold values from -0.25 to 0.25
- in_bias: float32 [64], replicated, may hold values from -3 to 3
- noise_embed: float32 [64], replicated, may hold values from -3 to 3
- norm_gain: float32 [64], replicated, may hold values from 0.5 to 2
Outputs:
- next_state: float32 [8, 2, 256, 256], P('tm', None, 'space')
Inputs may be any that keep to these rules, and one draw needn't show every extreme that they name: `station_owner`: among the stations of one device (each aligned block of 128 stations) at most 32 have the same owner strip; every strip owns some station.
All inputs are finite; a program needn't handle non-finite values.
Results may differ from a plain program's by a relative error of at most 0.0023.
Values may be sent and summed in bfloat16 or wider, within the bound.
A program may use at most 64 MiB of HBM per device.

v0:
```python
import jax
import jax.numpy as jnp
from jax import lax
from jax.sharding import PartitionSpec as P

WIN = 8
LEVELS = 32
STRIDE = 4
CHAN = 16


def extended_2(cells, sides, width):
    for axis, dim in sides:
        count = lax.axis_size(axis)
        head = lax.slice_in_dim(cells, 0, width, axis=dim)
        tail = lax.slice_in_dim(cells, cells.shape[dim] - width, cells.shape[dim], axis=dim)
        cells = jnp.concatenate(
            [
                lax.ppermute(tail, axis, [(i, (i + 1) % count) for i in range(count)]),
                cells,
                lax.ppermute(head, axis, [((i + 1) % count, i) for i in range(count)]),
            ],
            axis=dim,
        )
    return cells


def shifted(value, axis, steps):
    count = lax.axis_size(axis)
    first, last = (max(0, -steps), min(count, count - steps))
    return lax.ppermute(value, axis, [(source, source + steps) for source in range(first, last)])


def scale_at(level):
    return 0.3 * jnp.exp(jnp.log(5.0) * level.astype(jnp.float32) / (LEVELS - 1))


def conv_rows(weight, padded):
    out_rows = padded.shape[2] - 2
    stacked = jnp.concatenate(
        [jnp.roll(padded, 1 - col_tap, axis=3) for col_tap in range(3)], axis=1
    )
    total = None
    for row_tap in range(3):
        product = jnp.einsum(
            "oc,ncyx->noyx",
            weight[row_tap],
            stacked[:, :, row_tap : row_tap + out_rows, :],
            preferred_element_type=jnp.float32,
        )
        total = product if total is None else total + product
    return total


def hidden_rim(hidden):
    return extended_2(hidden, (("space", 2),), 1)


def score_net(windows, conv_in, conv_mid, conv_res, conv_out, bias, norm_gain):
    source = extended_2(windows, (("space", 2),), 1)
    first = jax.nn.silu(conv_rows(conv_in, source) + bias[None, :, None, None]).astype(jnp.bfloat16)
    middle = conv_rows(conv_mid, hidden_rim(first))
    normed = (
        middle
        * lax.rsqrt(jnp.mean(middle * middle, axis=1, keepdims=True) + 1e-05)
        * norm_gain[None, :, None, None]
    )
    second = jax.nn.silu(normed).astype(jnp.bfloat16)
    branch = jax.nn.silu(conv_rows(conv_res, hidden_rim(second)))
    third = (first.astype(jnp.float32) + branch).astype(jnp.bfloat16)
    return conv_rows(conv_out, hidden_rim(third))


def local(
    noisy_state,
    fresh_noise,
    level_index,
    station_obs,
    obs_variance,
    station_owner,
    station_cell,
    conv_in,
    conv_mid,
    conv_res,
    conv_out,
    in_bias,
    noise_embed,
    norm_gain,
):
    step_count, layer_count, row_count, col_count = noisy_state.shape
    noise_scale = scale_at(level_index[0])
    next_scale = scale_at(level_index[0] - 1)
    bias = in_bias + noise_embed * jnp.log(10.0 * noise_scale)
    scaled = (noisy_state / jnp.sqrt(1.0 + noise_scale * noise_scale)).astype(jnp.bfloat16)
    time_rank = lax.axis_index("tm")
    total_steps = step_count * lax.axis_size("tm")
    ahead = shifted(scaled, "tm", -1)
    extended = jnp.concatenate([scaled, ahead], axis=0)
    offset = 0
    window_count = (extended.shape[0] - WIN) // STRIDE + 1
    windows = jnp.stack([extended])
    windows = windows.reshape(window_count, CHAN, row_count, col_count)
    outputs = score_net(windows, conv_in, conv_mid, conv_res, conv_out, bias, norm_gain)
    starts = time_rank * step_count - offset + STRIDE * jnp.arange(window_count, dtype=jnp.int32)
    usable = ((starts >= 0) & (starts + WIN <= total_steps)).astype(jnp.float32)
    halves = (
        outputs.reshape(window_count, 2, STRIDE, layer_count, row_count, col_count)
        * usable[:, None, None, None, None, None]
    )
    blank = jnp.zeros((1, STRIDE, layer_count, row_count, col_count), jnp.float32)
    summed = jnp.concatenate([halves[:, 0], blank], axis=0) + jnp.concatenate(
        [blank, halves[:, 1]], axis=0
    )
    summed = summed.reshape(extended.shape[0], layer_count, row_count, col_count)
    spill = shifted(summed[step_count:], "tm", 1)
    own = jnp.concatenate([summed[:STRIDE] + spill, summed[STRIDE:step_count]], axis=0)
    moment = time_rank * step_count + jnp.arange(step_count, dtype=jnp.int32)
    cover = jnp.where((moment < STRIDE) | (moment >= total_steps - STRIDE), 1.0, 2.0).astype(
        jnp.float32
    )
    estimate = noisy_state - noise_scale * (own / cover[:, None, None, None])
    space_size = lax.axis_size("space")
    station_count = station_cell.shape[0]
    capacity = 4 * station_count // space_size
    values = station_obs.reshape(step_count * layer_count, station_count)
    target = station_owner[:, 0]
    earlier = lax.broadcasted_iota(
        jnp.int32, (station_count, station_count), 0
    ) < lax.broadcasted_iota(jnp.int32, (station_count, station_count), 1)
    ranked = jnp.sum(
        jnp.where((target[:, None] == target[None, :]) & earlier, 1, 0), axis=0
    ).astype(jnp.int32)
    slot = target * capacity + ranked
    slot_count = space_size * capacity
    value_slots = jnp.zeros((values.shape[0], slot_count), jnp.float32).at[:, slot].set(values)
    spread_slots = jnp.zeros((1, slot_count), jnp.float32).at[0, slot].set(obs_variance)
    cell_slots = jnp.full((1, slot_count), -1, jnp.int32).at[0, slot].set(station_cell)
    got_values, got_spread, got_cells = (
        lax.all_to_all(value_slots, "space", split_axis=1, concat_axis=1, tiled=True),
        lax.all_to_all(spread_slots, "space", split_axis=1, concat_axis=1, tiled=True),
        lax.all_to_all(cell_slots, "space", split_axis=1, concat_axis=1, tiled=True),
    )
    present = got_cells[0] >= 0
    spot = jnp.maximum(got_cells[0], 0)
    flat = estimate.reshape(step_count * layer_count, row_count * col_count)
    seen = jnp.take(flat, spot, axis=1)
    misfit = jnp.where(
        present[None, :], (got_values - seen) / (got_spread + noise_scale * noise_scale), 0.0
    )
    pull = jnp.zeros_like(flat).at[:, spot].add(misfit)
    return (
        estimate
        + noise_scale * noise_scale * pull.reshape(estimate.shape)
        + next_scale * fresh_noise
    )


def solution(mesh):
    placed = (
        P("tm", None, "space", None),
        P("tm", None, "space", None),
        P(),
        P("tm", None, "space"),
        P("space"),
        P("space", None),
        P("space"),
        P(),
        P(),
        P(),
        P(),
        P(),
        P(),
        P(),
    )
    return jax.shard_map(
        local, mesh=mesh, in_specs=placed, out_specs=P("tm", None, "space", None), check_vma=False
    )
```

profile of v0, /device:TPU:0, one launch (start us, length us, event | category | flops | bytes accessed | tf_op | source)
XLA Modules:
  0.0 83.0 jit_solution(5439972341782676317)
XLA Ops:
  0.8 0.9 %divide_convert_fusion = bf16[4,2,16,256]{3,2,1,0:T(8,128)(2,1)S(1)} fusion(f32[4,2,16,256]{3,2,1,0:T(8,128)} %param.14, f32[]{:T(128)S(6)} %sqrt.3), kind=kLoop, calls=%fused_computation.84 | loop fusion | flops 65536 | bytes 196612 | tf_op jit(solution)/shard_map/convert_element_type | solution.py:94
  1.7 1.3 %collective-permute-start = (bf16[4,2,16,256]{3,2,1,0:T(8,128)(2,1)S(1)}, bf16[4,2,16,256]{3,2,1,0:T(8,128)(2,1)S(1)}, u32[]{:S(2)}, u32[]{:S(2)}) collective-permute-start(bf16[4,2,16,256]{3,2,1,0:T(8,128)(2,1)S(1)} %divide_convert_fusion), channel_id=1, source_target_pairs={{16,0},{17,1},{18,2},{19,3},{20,4},{21,5},{22,6},{23,7},{24,8},{25... | collective-permute-start | bytes 196616 | tf_op jit(solution)/shard_map/ppermute | solution.py:31
  3.0 0.8 select_reduce_fusion
  4.5 1.1 %scatter_custom_fusion = s32[512]{0:T(512)S(1)} fusion(s32[128]{0:T(128)S(1)} %fusion.78, s32[128]{0:T(128)} %param.20, s32[]{:T(128)} %constant.78.clone.1), kind=kCustom, calls=%fused_computation.129 | custom fusion | bytes 2560 | tf_op jit(solution)/shard_map/scatter | solution.py:137
  6.3 7.4 %all-to-all-start = ((s32[1,16,32]{2,0,1:T(1,128)}), s32[1,16,32]{2,0,1:T(1,128)S(1)}, u32[]{:S(2)}, u32[]{:S(2)}) async-start(s32[1,16,32]{2,0,1:T(1,128)} %all_to_all.20), calls=%async_computation | async-start | bytes 16384 | tf_op jit(solution)/shard_map/all_to_all | solution.py:141
  14.9 4.1 %collective-permute-start.2 = (bf16[1,16,1,256]{3,1,2,0:T(8,128)(2,1)S(1)}, bf16[1,16,1,256]{3,1,2,0:T(8,128)(2,1)S(1)}, u32[]{:S(2)}, u32[]{:S(2)}) collective-permute-start(bf16[1,16,1,256]{3,1,2,0:T(8,128)(2,1)S(1)} %copy.65), channel_id=1, source_target_pairs={{1,0},{2,1},{3,2},{4,3},{5,4},{6,5},{7,6},{8,7},{9,8},{10,9},{11,1... | collective-permute-start | bytes 24584 | tf_op jit(solution)/shard_map/ppermute | solution.py:21
  19.7 0.7 collective-permute-done.2
  22.0 4.5 %collective-permute-start.4 = (bf16[1,64,1,256]{3,1,2,0:T(8,128)(2,1)S(1)}, bf16[1,64,1,256]{3,1,2,0:T(8,128)(2,1)S(1)}, u32[]{:S(2)}, u32[]{:S(2)}) collective-permute-start(bf16[1,64,1,256]{3,1,2,0:T(8,128)(2,1)S(1)} %get-tuple-element.24), channel_id=1, source_target_pairs={{1,0},{2,1},{3,2},{4,3},{5,4},{6,5},{7,6},{8,7},{9,8},{10,9},{11,1... | collective-permute-start | bytes 98312 | tf_op jit(solution)/shard_map/ppermute | solution.py:21
  26.5 1.1 %scatter_custom_fusion.2 = f32[512]{0:T(512)S(1)} fusion(s32[128]{0:T(128)S(1)} %fusion.78, f32[128]{0:T(128)} %param.18, f32[]{:T(128)} %constant.35.clone.1), kind=kCustom, calls=%fused_computation.127 | custom fusion | bytes 2560 | tf_op jit(solution)/shard_map/scatter | solution.py:136
  28.4 0.9 %scatter_custom_fusion.1 = f32[8,512]{0,1:T(8,128)S(1)} fusion(s32[128]{0:T(128)S(1)} %fusion.78, f32[]{:T(128)} %constant.35.clone.1, f32[8,128]{0,1:T(8,128)S(1)} %copy.54), kind=kCustom, calls=%fused_computation.82 | custom fusion | bytes 81924 | tf_op jit(solution)/shard_map/scatter | solution.py:135
  29.5 0.7 reshape.297
  30.8 1.4 %maximum_maximum_fusion = bf16[1,192,18,256]{3,1,2,0:T(8,128)(2,1)S(1)} fusion(bf16[1,64,18,1]{3,1,2,0:T(8,128)(2,1)S(1)} %get-tuple-element.16, bf16[1,64,18,255]{3,1,2,0:T(8,128)(2,1)S(1)} %get-tuple-element.18, bf16[1,64,1,256]{3,1,2,0:T(8,128)(2,1)S(1)} %collective-permute-done.4, bf16[1,64,16,256]{3,1,2,0:T(8,128)(2,1)S(1)} %multiply_convert_fusion, ...), kind=kLoop, calls=%fused_computation.5 | loop fusion | flops 12386304 | bytes 3538944 | tf_op jit(solution)/shard_map/concatenate | solution.py:40
  34.2 4.4 %collective-permute-start.6 = (bf16[1,64,1,256]{3,1,2,0:T(8,128)(2,1)S(1)}, bf16[1,64,1,256]{3,1,2,0:T(8,128)(2,1)S(1)}, u32[]{:S(2)}, u32[]{:S(2)}) collective-permute-start(bf16[1,64,1,256]{3,1,2,0:T(8,128)(2,1)S(1)} %get-tuple-element.22), channel_id=1, source_target_pairs={{1,0},{2,1},{3,2},{4,3},{5,4},{6,5},{7,6},{8,7},{9,8},{10,9},{11,1... | collective-permute-start | bytes 98312 | tf_op jit(solution)/shard_map/ppermute | solution.py:21
  38.6 3.4 %all-to-all-start.2 = ((f32[1,16,32]{2,0,1:T(1,128)}), f32[1,16,32]{2,0,1:T(1,128)S(1)}, u32[]{:S(2)}, u32[]{:S(2)}) async-start(f32[1,16,32]{2,0,1:T(1,128)} %all_to_all.25), calls=%async_computation.2 | async-start | bytes 16384 | tf_op jit(solution)/shard_map/all_to_all | solution.py:140
  42.7 1.4 %maximum_maximum_fusion.1 = bf16[1,192,18,256]{3,1,2,0:T(8,128)(2,1)S(1)} fusion(bf16[1,64,18,1]{3,1,2,0:T(8,128)(2,1)S(1)} %get-tuple-element.12, bf16[1,64,18,255]{3,1,2,0:T(8,128)(2,1)S(1)} %get-tuple-element.14, bf16[1,64,1,256]{3,1,2,0:T(8,128)(2,1)S(1)} %collective-permute-done.6, bf16[1,64,16,256]{3,1,2,0:T(8,128)(2,1)S(1)} %fusion.27, ...), kind=kLoop, calls=%fused_computation.6 | loop fusion | flops 12386304 | bytes 3538944 | tf_op jit(solution)/shard_map/concatenate | solution.py:40
  45.9 4.2 %collective-permute-start.8 = (bf16[1,64,1,256]{3,1,2,0:T(8,128)(2,1)S(1)}, bf16[1,64,1,256]{3,1,2,0:T(8,128)(2,1)S(1)}, u32[]{:S(2)}, u32[]{:S(2)}) collective-permute-start(bf16[1,64,1,256]{3,1,2,0:T(8,128)(2,1)S(1)} %get-tuple-element.20), channel_id=1, source_target_pairs={{1,0},{2,1},{3,2},{4,3},{5,4},{6,5},{7,6},{8,7},{9,8},{10,9},{11,1... | collective-permute-start | bytes 98312 | tf_op jit(solution)/shard_map/ppermute | solution.py:21
  50.1 1.6 %collective-permute-done.7 = bf16[1,64,1,256]{3,1,2,0:T(8,128)(2,1)S(1)} collective-permute-done((bf16[1,64,1,256]{3,1,2,0:T(8,128)(2,1)S(1)}, bf16[1,64,1,256]{3,1,2,0:T(8,128)(2,1)S(1)}, u32[]{:S(2)}, u32[]{:S(2)}) %collective-permute-start.7) | collective-permute-done | bytes 32800 | tf_op jit(solution)/shard_map/ppermute | solution.py:19
  52.2 1.4 %maximum_maximum_fusion.2 = bf16[1,192,18,256]{3,1,2,0:T(8,128)(2,1)S(1)} fusion(bf16[1,64,18,1]{3,1,2,0:T(8,128)(2,1)S(1)} %get-tuple-element.8, bf16[1,64,18,255]{3,1,2,0:T(8,128)(2,1)S(1)} %get-tuple-element.10, bf16[1,64,1,256]{3,1,2,0:T(8,128)(2,1)S(1)} %collective-permute-done.8, bf16[1,64,16,256]{3,1,2,0:T(8,128)(2,1)S(1)} %add_convert_fusion, ...), kind=kLoop, calls=%fused_computation.7 | loop fusion | flops 12386304 | bytes 3538944 | tf_op jit(solution)/shard_map/concatenate | solution.py:40
  54.8 4.5 %collective-permute-start.9 = (f32[4,2,16,256]{3,2,1,0:T(8,128)S(1)}, f32[4,2,16,256]{3,2,1,0:T(8,128)S(1)}, u32[]{:S(2)}, u32[]{:S(2)}) collective-permute-start(f32[4,2,16,256]{3,2,1,0:T(8,128)S(1)} %fusion.40), channel_id=1, source_target_pairs={{0,16},{1,17},{2,18},{3,19},{4,20},{5,21},{6,22},{7,23},{8,24},{9,... | collective-permute-start | bytes 393224 | tf_op jit(solution)/shard_map/ppermute | solution.py:31
  59.3 5.6 %all-to-all-start.1 = ((f32[16,1,256]{2,1,0:T(1,128)}), f32[16,1,256]{2,1,0:T(1,128)S(1)}, u32[]{:S(2)}, u32[]{:S(2)}) async-start(f32[16,1,256]{2,1,0:T(1,128)} %reshape.297), calls=%async_computation.1 | async-start | bytes 32768 | tf_op jit(solution)/shard_map/all_to_all | solution.py:139
  65.3 6.1 %all-to-all-done.1 = f32[16,1,256]{2,1,0:T(1,128)S(1)} async-done(((f32[16,1,256]{2,1,0:T(1,128)}), f32[16,1,256]{2,1,0:T(1,128)S(1)}, u32[]{:S(2)}, u32[]{:S(2)}) %all-to-all-start.1) | async-done | bytes 16416 | tf_op jit(solution)/shard_map/all_to_all | solution.py:139
  73.6 6.4 %scatter_custom_fusion.3 = f32[8,4096]{0,1:T(8,128)} fusion(s32[512]{0:T(512)S(1)} %reshape.243, f32[]{:T(128)} %constant.35.clone.1, f32[8,512]{0,1:T(8,128)S(1)} %bitcast.203, f32[]{:T(128)} %constant.83.clone.1, f32[512]{0:T(512)S(1)} %add.188, pred[512]{0:T(512)(128)(4,1)S(1)} %le.21, pred[512]{0:T(512)(128)(4,1)S(1)} %ge.31, f32[8,4096]{0,1:T(8,128)S(1)} %copy.57, ...), kind=kCustom, calls=%fused_computation.46 | custom fusion | flops 20480 | bytes 2499072 | tf_op jit(solution)/shard_map/scatter-add | solution.py:150
  80.0 2.2 %copy.58 = f32[8,4096]{1,0:T(8,128)S(1)} copy(f32[8,4096]{0,1:T(8,128)} %scatter_custom_fusion.3) | data formatting | bytes 262144 | tf_op jit(solution)/shard_map/scatter-add | solution.py:150
  82.3 0.7 multiply_add_fusion
  (93 shorter events, 14.9 us)
Async XLA Ops:
  0.0 20.7 %copy-start.5 = (bf16[3,64,48]{1,2,0:T(8,128)(2,1)S(1)}, bf16[3,64,48]{1,2,0:T(8,128)(2,1)}, u32[]{:S(2)}) copy-start(bf16[3,64,48]{1,2,0:T(8,128)(2,1)} %param.21) | copy-start | bytes 55300
  1.7 12.0 %collective-permute-start = (bf16[4,2,16,256]{3,2,1,0:T(8,128)(2,1)S(1)}, bf16[4,2,16,256]{3,2,1,0:T(8,128)(2,1)S(1)}, u32[]{:S(2)}, u32[]{:S(2)}) collective-permute-start(bf16[4,2,16,256]{3,2,1,0:T(8,128)(2,1)S(1)} %divide_convert_fusion), channel_id=1, source_target_pairs={{16,0},{17,1},{18,2},{19,3},{20,4},{21,5},{22,6},{23,7},{24,8},{25... | collective-permute-start | bytes 196616 | tf_op jit(solution)/shard_map/ppermute | solution.py:31
  6.3 32.3 %all-to-all-start = ((s32[1,16,32]{2,0,1:T(1,128)}), s32[1,16,32]{2,0,1:T(1,128)S(1)}, u32[]{:S(2)}, u32[]{:S(2)}) async-start(s32[1,16,32]{2,0,1:T(1,128)} %all_to_all.20), calls=%async_computation | async-start | bytes 16384 | tf_op jit(solution)/shard_map/all_to_all | solution.py:141
  13.8 5.8 %collective-permute-start.1 = (bf16[1,16,1,256]{3,1,2,0:T(8,128)(2,1)S(1)}, bf16[1,16,1,256]{3,1,2,0:T(8,128)(2,1)S(1)}, u32[]{:S(2)}, u32[]{:S(2)}) collective-permute-start(bf16[1,16,1,256]{3,1,2,0:T(8,128)(2,1)S(1)} %copy.64), channel_id=1, source_target_pairs={{0,1},{1,2},{2,3},{3,4},{4,5},{5,6},{6,7},{7,8},{8,9},{9,10},{10,1... | collective-permute-start | bytes 24584 | tf_op jit(solution)/shard_map/ppermute | solution.py:19
  14.9 5.4 %collective-permute-start.2 = (bf16[1,16,1,256]{3,1,2,0:T(8,128)(2,1)S(1)}, bf16[1,16,1,256]{3,1,2,0:T(8,128)(2,1)S(1)}, u32[]{:S(2)}, u32[]{:S(2)}) collective-permute-start(bf16[1,16,1,256]{3,1,2,0:T(8,128)(2,1)S(1)} %copy.65), channel_id=1, source_target_pairs={{1,0},{2,1},{3,2},{4,3},{5,4},{6,5},{7,6},{8,7},{9,8},{10,9},{11,1... | collective-permute-start | bytes 24584 | tf_op jit(solution)/shard_map/ppermute | solution.py:21
  21.4 6.9 %copy-start.6 = (f32[4,2,128]{2,1,0:T(2,128)S(1)}, f32[4,2,128]{2,1,0:T(2,128)}, u32[]{:S(2)}) copy-start(f32[4,2,128]{2,1,0:T(2,128)} %param.17) | copy-start | bytes 12292
  22.0 8.3 %collective-permute-start.3 = (bf16[1,64,1,256]{3,1,2,0:T(8,128)(2,1)S(1)}, bf16[1,64,1,256]{3,1,2,0:T(8,128)(2,1)S(1)}, u32[]{:S(2)}, u32[]{:S(2)}) collective-permute-start(bf16[1,64,1,256]{3,1,2,0:T(8,128)(2,1)S(1)} %get-tuple-element.23), channel_id=1, source_target_pairs={{0,1},{1,2},{2,3},{3,4},{4,5},{5,6},{6,7},{7,8},{8,9},{9,10},{10,1... | collective-permute-start | bytes 98312 | tf_op jit(solution)/shard_map/ppermute | solution.py:19
  22.0 8.2 %collective-permute-start.4 = (bf16[1,64,1,256]{3,1,2,0:T(8,128)(2,1)S(1)}, bf16[1,64,1,256]{3,1,2,0:T(8,128)(2,1)S(1)}, u32[]{:S(2)}, u32[]{:S(2)}) collective-permute-start(bf16[1,64,1,256]{3,1,2,0:T(8,128)(2,1)S(1)} %get-tuple-element.24), channel_id=1, source_target_pairs={{1,0},{2,1},{3,2},{4,3},{5,4},{6,5},{7,6},{8,7},{9,8},{10,9},{11,1... | collective-permute-start | bytes 98312 | tf_op jit(solution)/shard_map/ppermute | solution.py:21
  30.8 1.4 %copy-start.2 = (bf16[3,64,192]{2,1,0:T(8,128)(2,1)S(1)}, bf16[3,64,192]{2,1,0:T(8,128)(2,1)}, u32[]{:S(2)}) copy-start(bf16[3,64,192]{2,1,0:T(8,128)(2,1)} %param.22) | copy-start | bytes 221188
  33.0 0.7 copy-start.7
  34.1 8.0 %collective-permute-start.5 = (bf16[1,64,1,256]{3,1,2,0:T(8,128)(2,1)S(1)}, bf16[1,64,1,256]{3,1,2,0:T(8,128)(2,1)S(1)}, u32[]{:S(2)}, u32[]{:S(2)}) collective-permute-start(bf16[1,64,1,256]{3,1,2,0:T(8,128)(2,1)S(1)} %get-tuple-element.21), channel_id=1, source_target_pairs={{0,1},{1,2},{2,3},{3,4},{4,5},{5,6},{6,7},{7,8},{8,9},{9,10},{10,1... | collective-permute-start | bytes 98312 | tf_op jit(solution)/shard_map/ppermute | solution.py:19
  34.2 8.0 %collective-permute-start.6 = (bf16[1,64,1,256]{3,1,2,0:T(8,128)(2,1)S(1)}, bf16[1,64,1,256]{3,1,2,0:T(8,128)(2,1)S(1)}, u32[]{:S(2)}, u32[]{:S(2)}) collective-permute-start(bf16[1,64,1,256]{3,1,2,0:T(8,128)(2,1)S(1)} %get-tuple-element.22), channel_id=1, source_target_pairs={{1,0},{2,1},{3,2},{4,3},{5,4},{6,5},{7,6},{8,7},{9,8},{10,9},{11,1... | collective-permute-start | bytes 98312 | tf_op jit(solution)/shard_map/ppermute | solution.py:21
  38.6 20.7 %all-to-all-start.2 = ((f32[1,16,32]{2,0,1:T(1,128)}), f32[1,16,32]{2,0,1:T(1,128)S(1)}, u32[]{:S(2)}, u32[]{:S(2)}) async-start(f32[1,16,32]{2,0,1:T(1,128)} %all_to_all.25), calls=%async_computation.2 | async-start | bytes 16384 | tf_op jit(solution)/shard_map/all_to_all | solution.py:140
  42.7 1.4 %copy-start.3 = (bf16[3,64,192]{2,1,0:T(8,128)(2,1)S(1)}, bf16[3,64,192]{2,1,0:T(8,128)(2,1)}, u32[]{:S(2)}) copy-start(bf16[3,64,192]{2,1,0:T(8,128)(2,1)} %param.23) | copy-start | bytes 221188
  45.5 6.1 %collective-permute-start.7 = (bf16[1,64,1,256]{3,1,2,0:T(8,128)(2,1)S(1)}, bf16[1,64,1,256]{3,1,2,0:T(8,128)(2,1)S(1)}, u32[]{:S(2)}, u32[]{:S(2)}) collective-permute-start(bf16[1,64,1,256]{3,1,2,0:T(8,128)(2,1)S(1)} %get-tuple-element.19), channel_id=1, source_target_pairs={{0,1},{1,2},{2,3},{3,4},{4,5},{5,6},{6,7},{7,8},{8,9},{9,10},{10,1... | collective-permute-start | bytes 98312 | tf_op jit(solution)/shard_map/ppermute | solution.py:19
  45.9 5.8 %collective-permute-start.8 = (bf16[1,64,1,256]{3,1,2,0:T(8,128)(2,1)S(1)}, bf16[1,64,1,256]{3,1,2,0:T(8,128)(2,1)S(1)}, u32[]{:S(2)}, u32[]{:S(2)}) collective-permute-start(bf16[1,64,1,256]{3,1,2,0:T(8,128)(2,1)S(1)} %get-tuple-element.20), channel_id=1, source_target_pairs={{1,0},{2,1},{3,2},{4,3},{5,4},{6,5},{7,6},{8,7},{9,8},{10,9},{11,1... | collective-permute-start | bytes 98312 | tf_op jit(solution)/shard_map/ppermute | solution.py:21
  52.2 1.4 %copy-start.4 = (bf16[3,16,192]{2,1,0:T(8,128)(2,1)S(1)}, bf16[3,16,192]{2,1,0:T(8,128)(2,1)}, u32[]{:S(2)}) copy-start(bf16[3,16,192]{2,1,0:T(8,128)(2,1)} %param.24) | copy-start | bytes 55300
  54.2 18.6 %copy-start = (f32[4,2,16,256]{3,2,1,0:T(8,128)S(1)}, f32[4,2,16,256]{3,2,1,0:T(8,128)}, u32[]{:S(2)}) copy-start(f32[4,2,16,256]{3,2,1,0:T(8,128)} %param.14) | copy-start | bytes 393220
  54.8 18.0 %collective-permute-start.9 = (f32[4,2,16,256]{3,2,1,0:T(8,128)S(1)}, f32[4,2,16,256]{3,2,1,0:T(8,128)S(1)}, u32[]{:S(2)}, u32[]{:S(2)}) collective-permute-start(f32[4,2,16,256]{3,2,1,0:T(8,128)S(1)} %fusion.40), channel_id=1, source_target_pairs={{0,16},{1,17},{2,18},{3,19},{4,20},{5,21},{6,22},{7,23},{8,24},{9,... | collective-permute-start | bytes 393224 | tf_op jit(solution)/shard_map/ppermute | solution.py:31
  59.3 12.1 %all-to-all-start.1 = ((f32[16,1,256]{2,1,0:T(1,128)}), f32[16,1,256]{2,1,0:T(1,128)S(1)}, u32[]{:S(2)}, u32[]{:S(2)}) async-start(f32[16,1,256]{2,1,0:T(1,128)} %reshape.297), calls=%async_computation.1 | async-start | bytes 32768 | tf_op jit(solution)/shard_map/all_to_all | solution.py:139
  80.0 2.3 %copy-start.1 = (f32[4,2,16,256]{3,2,1,0:T(8,128)S(1)}, f32[4,2,16,256]{3,2,1,0:T(8,128)}, u32[]{:S(2)}) copy-start(f32[4,2,16,256]{3,2,1,0:T(8,128)} %param.15) | copy-start | bytes 393220
where the time goes:
time: 83.5 us; the launch traced here: 83 us
  starting transfers between devices  40.3 us (48%)
  other arithmetic  16 us (19%)
  local copies, waits for them, and re-layouts  11.5 us (14%)
  waiting for transfers between devices  9.03 us (11%)
  matrix products  4.83 us (6%)
  between operations  1.38 us (2%)
    ppermute x4, starting transfers between devices, extended_2(): lax.ppermute(head, axis, [((i + 1) % count, i) for i in range(count)])  17.1 us
    all_to_all x1, starting transfers between devices, local(): lax.all_to_all(cell_slots, 'space', split_axis=1, concat_axis=1, tiled=True)  7.39 us
    scatter-add x1, other arithmetic, local(): pull = jnp.zeros_like(flat).at[:, spot].add(misfit)  6.41 us
    all_to_all x1, waiting for transfers between devices, local(): lax.all_to_all(value_slots, 'space', split_axis=1, concat_axis=1, tiled=T...  6.12 us
    ppermute x2, starting transfers between devices, shifted(): lax.ppermute(value, axis, [(source, source + steps) for source in range(f...  5.84 us
    all_to_all x1, starting transfers between devices, local(): lax.all_to_all(value_slots, 'space', split_axis=1, concat_axis=1, tiled=T...  5.56 us
    dot_general x12, matrix products, conv_rows(): jnp.einsum('oc,ncyx->noyx', weight[row_tap], stacked[:, :, row_tap:row_ta...  4.83 us
    concatenate x4, other arithmetic, conv_rows(): jnp.concatenate([jnp.roll(padded, 1 - col_tap, axis=3) for col_tap in ran...  4.2 us
  transfers between devices with their start and end apart: 13, of which 4 were waited for; matrix products, arithmetic and copies ran while one was open for 24% of the time, Pallas kernels for 0%

commit v1 on v0

--- a/solution.py
+++ b/solution.py
@@ -138,7 +138,12 @@
     got_values, got_spread, got_cells = (
         lax.all_to_all(value_slots, "space", split_axis=1, concat_axis=1, tiled=True),
         lax.all_to_all(spread_slots, "space", split_axis=1, concat_axis=1, tiled=True),
-        lax.all_to_all(cell_slots, "space", split_axis=1, concat_axis=1, tiled=True),
+        jnp.concatenate(
+            lax.all_to_all(
+                jnp.stack(jnp.split(cell_slots, lax.axis_size("space"), axis=1)), "space", 0, 0
+            ),
+            axis=1,
+        ),
     )
     present = got_cells[0] >= 0
     spot = jnp.maximum(got_cells[0], 0)

time: 83.5 us -> 92.4 us (1.11)
  local copies, waits for them, and re-layouts: 11.5 us -> 20.4 us
    unnamed x24 -> x39, local copies, waits for them, and re-layouts: 1.17 us -> 10.1 us
  transfers between devices with their start and end apart: 13 -> 13, of which waited for: 4 -> 4; matrix products, arithmetic and copies ran while one was open for 24% -> 32% of each run, Pallas kernels for 0% -> 0%
where the time goes in v1:
time: 92.4 us; the launch traced here: 92 us
  starting transfers between devices  40.3 us (44%)
  local copies, waits for them, and re-layouts  20.4 us (22%)
  other arithmetic  16 us (17%)
  waiting for transfers between devices  9.03 us (10%)
  matrix products  4.82 us (5%)
  between operations  1.39 us (2%)
    ppermute x4, starting transfers between devices, extended_2(): lax.ppermute(head, axis, [((i + 1) % count, i) for i in range(count)])  17.1 us
    unnamed x39, local copies, waits for them, and re-layouts  10.1 us
    all_to_all x1, starting transfers between devices, local(): lax.all_to_all(jnp.stack(jnp.split(cell_slots, lax.axis_size('space'), ax...  7.39 us
    scatter-add x1, other arithmetic, local(): pull = jnp.zeros_like(flat).at[:, spot].add(misfit)  6.41 us
    all_to_all x1, waiting for transfers between devices, local(): lax.all_to_all(value_slots, 'space', split_axis=1, concat_axis=1, tiled=T...  6.12 us
    ppermute x2, starting transfers between devices, shifted(): lax.ppermute(value, axis, [(source, source + steps) for source in range(f...  5.84 us
    all_to_all x1, starting transfers between devices, local(): lax.all_to_all(value_slots, 'space', split_axis=1, concat_axis=1, tiled=T...  5.56 us
    dot_general x12, matrix products, conv_rows(): jnp.einsum('oc,ncyx->noyx', weight[row_tap], stacked[:, :, row_tap:row_ta...  4.82 us
  transfers between devices with their start and end apart: 13, of which 4 were waited for; matrix products, arithmetic and copies ran while one was open for 32% of the time, Pallas kernels for 0%

profile of v1, /device:TPU:0, one launch (start us, length us, event | category | flops | bytes accessed | tf_op | source)
XLA Modules:
  0.0 92.0 jit_solution(17451010230379906396)
XLA Ops:
  0.8 0.9 %divide_convert_fusion = bf16[4,2,16,256]{3,2,1,0:T(8,128)(2,1)S(1)} fusion(f32[4,2,16,256]{3,2,1,0:T(8,128)} %param.14, f32[]{:T(128)S(6)} %sqrt.3), kind=kLoop, calls=%fused_computation.84 | loop fusion | flops 65536 | bytes 196612 | tf_op jit(solution)/shard_map/convert_element_type | solution.py:94
  1.7 1.3 %collective-permute-start = (bf16[4,2,16,256]{3,2,1,0:T(8,128)(2,1)S(1)}, bf16[4,2,16,256]{3,2,1,0:T(8,128)(2,1)S(1)}, u32[]{:S(2)}, u32[]{:S(2)}) collective-permute-start(bf16[4,2,16,256]{3,2,1,0:T(8,128)(2,1)S(1)} %divide_convert_fusion), channel_id=1, source_target_pairs={{16,0},{17,1},{18,2},{19,3},{20,4},{21,5},{22,6},{23,7},{24,8},{25... | collective-permute-start | bytes 196616 | tf_op jit(solution)/shard_map/ppermute | solution.py:31
  3.0 0.8 select_reduce_fusion
  4.5 1.1 %scatter_custom_fusion = s32[512]{0:T(512)S(1)} fusion(s32[128]{0:T(128)S(1)} %fusion.78, s32[128]{0:T(128)} %param.20, s32[]{:T(128)} %constant.78.clone.1), kind=kCustom, calls=%fused_computation.145 | custom fusion | bytes 2560 | tf_op jit(solution)/shard_map/scatter | solution.py:137
  15.2 7.4 %all-to-all-start = ((s32[16,1,32]{2,1,0:T(1,128)}), s32[16,1,32]{2,1,0:T(1,128)S(1)}, u32[]{:S(2)}, u32[]{:S(2)}) async-start(s32[16,1,32]{2,1,0:T(1,128)} %constant_dynamic-update-slice_fusion.3), calls=%async_computation | async-start | bytes 16384 | tf_op jit(solution)/shard_map/all_to_all | solution.py:142
  23.9 4.1 %collective-permute-start.2 = (bf16[1,16,1,256]{3,1,2,0:T(8,128)(2,1)S(1)}, bf16[1,16,1,256]{3,1,2,0:T(8,128)(2,1)S(1)}, u32[]{:S(2)}, u32[]{:S(2)}) collective-permute-start(bf16[1,16,1,256]{3,1,2,0:T(8,128)(2,1)S(1)} %copy.57), channel_id=1, source_target_pairs={{1,0},{2,1},{3,2},{4,3},{5,4},{6,5},{7,6},{8,7},{9,8},{10,9},{11,1... | collective-permute-start | bytes 24584 | tf_op jit(solution)/shard_map/ppermute | solution.py:21
  28.6 0.7 collective-permute-done.2
  30.9 4.5 %collective-permute-start.4 = (bf16[1,64,1,256]{3,1,2,0:T(8,128)(2,1)S(1)}, bf16[1,64,1,256]{3,1,2,0:T(8,128)(2,1)S(1)}, u32[]{:S(2)}, u32[]{:S(2)}) collective-permute-start(bf16[1,64,1,256]{3,1,2,0:T(8,128)(2,1)S(1)} %get-tuple-element.24), channel_id=1, source_target_pairs={{1,0},{2,1},{3,2},{4,3},{5,4},{6,5},{7,6},{8,7},{9,8},{10,9},{11,1... | collective-permute-start | bytes 98312 | tf_op jit(solution)/shard_map/ppermute | solution.py:21
  35.4 1.1 %scatter_custom_fusion.2 = f32[512]{0:T(512)S(1)} fusion(s32[128]{0:T(128)S(1)} %fusion.78, f32[128]{0:T(128)} %param.18, f32[]{:T(128)} %constant.35.clone.1), kind=kCustom, calls=%fused_computation.143 | custom fusion | bytes 2560 | tf_op jit(solution)/shard_map/scatter | solution.py:136
  37.3 0.9 %scatter_custom_fusion.1 = f32[8,512]{0,1:T(8,128)S(1)} fusion(s32[128]{0:T(128)S(1)} %fusion.78, f32[]{:T(128)} %constant.35.clone.1, f32[8,128]{0,1:T(8,128)S(1)} %copy.46), kind=kCustom, calls=%fused_computation.82 | custom fusion | bytes 81924 | tf_op jit(solution)/shard_map/scatter | solution.py:135
  38.4 0.7 reshape.293
  39.8 1.4 %maximum_maximum_fusion = bf16[1,192,18,256]{3,1,2,0:T(8,128)(2,1)S(1)} fusion(bf16[1,64,18,1]{3,1,2,0:T(8,128)(2,1)S(1)} %get-tuple-element.16, bf16[1,64,18,255]{3,1,2,0:T(8,128)(2,1)S(1)} %get-tuple-element.18, bf16[1,64,1,256]{3,1,2,0:T(8,128)(2,1)S(1)} %collective-permute-done.4, bf16[1,64,16,256]{3,1,2,0:T(8,128)(2,1)S(1)} %multiply_convert_fusion, ...), kind=kLoop, calls=%fused_computation.5 | loop fusion | flops 12386304 | bytes 3538944 | tf_op jit(solution)/shard_map/concatenate | solution.py:40
  43.1 4.4 %collective-permute-start.6 = (bf16[1,64,1,256]{3,1,2,0:T(8,128)(2,1)S(1)}, bf16[1,64,1,256]{3,1,2,0:T(8,128)(2,1)S(1)}, u32[]{:S(2)}, u32[]{:S(2)}) collective-permute-start(bf16[1,64,1,256]{3,1,2,0:T(8,128)(2,1)S(1)} %get-tuple-element.22), channel_id=1, source_target_pairs={{1,0},{2,1},{3,2},{4,3},{5,4},{6,5},{7,6},{8,7},{9,8},{10,9},{11,1... | collective-permute-start | bytes 98312 | tf_op jit(solution)/shard_map/ppermute | solution.py:21
  47.5 3.5 %all-to-all-start.2 = ((f32[1,16,32]{2,0,1:T(1,128)}), f32[1,16,32]{2,0,1:T(1,128)S(1)}, u32[]{:S(2)}, u32[]{:S(2)}) async-start(f32[1,16,32]{2,0,1:T(1,128)} %all_to_all.21), calls=%async_computation.2 | async-start | bytes 16384 | tf_op jit(solution)/shard_map/all_to_all | solution.py:140
  51.7 1.4 %maximum_maximum_fusion.1 = bf16[1,192,18,256]{3,1,2,0:T(8,128)(2,1)S(1)} fusion(bf16[1,64,18,1]{3,1,2,0:T(8,128)(2,1)S(1)} %get-tuple-element.12, bf16[1,64,18,255]{3,1,2,0:T(8,128)(2,1)S(1)} %get-tuple-element.14, bf16[1,64,1,256]{3,1,2,0:T(8,128)(2,1)S(1)} %collective-permute-done.6, bf16[1,64,16,256]{3,1,2,0:T(8,128)(2,1)S(1)} %fusion.27, ...), kind=kLoop, calls=%fused_computation.6 | loop fusion | flops 12386304 | bytes 3538944 | tf_op jit(solution)/shard_map/concatenate | solution.py:40
  54.8 4.2 %collective-permute-start.8 = (bf16[1,64,1,256]{3,1,2,0:T(8,128)(2,1)S(1)}, bf16[1,64,1,256]{3,1,2,0:T(8,128)(2,1)S(1)}, u32[]{:S(2)}, u32[]{:S(2)}) collective-permute-start(bf16[1,64,1,256]{3,1,2,0:T(8,128)(2,1)S(1)} %get-tuple-element.20), channel_id=1, source_target_pairs={{1,0},{2,1},{3,2},{4,3},{5,4},{6,5},{7,6},{8,7},{9,8},{10,9},{11,1... | collective-permute-start | bytes 98312 | tf_op jit(solution)/shard_map/ppermute | solution.py:21
  59.0 1.6 %collective-permute-done.7 = bf16[1,64,1,256]{3,1,2,0:T(8,128)(2,1)S(1)} collective-permute-done((bf16[1,64,1,256]{3,1,2,0:T(8,128)(2,1)S(1)}, bf16[1,64,1,256]{3,1,2,0:T(8,128)(2,1)S(1)}, u32[]{:S(2)}, u32[]{:S(2)}) %collective-permute-start.7) | collective-permute-done | bytes 32800 | tf_op jit(solution)/shard_map/ppermute | solution.py:19
  61.2 1.4 %maximum_maximum_fusion.2 = bf16[1,192,18,256]{3,1,2,0:T(8,128)(2,1)S(1)} fusion(bf16[1,64,18,1]{3,1,2,0:T(8,128)(2,1)S(1)} %get-tuple-element.8, bf16[1,64,18,255]{3,1,2,0:T(8,128)(2,1)S(1)} %get-tuple-element.10, bf16[1,64,1,256]{3,1,2,0:T(8,128)(2,1)S(1)} %collective-permute-done.8, bf16[1,64,16,256]{3,1,2,0:T(8,128)(2,1)S(1)} %add_convert_fusion, ...), kind=kLoop, calls=%fused_computation.7 | loop fusion | flops 12386304 | bytes 3538944 | tf_op jit(solution)/shard_map/concatenate | solution.py:40
  63.7 4.5 %collective-permute-start.9 = (f32[4,2,16,256]{3,2,1,0:T(8,128)S(1)}, f32[4,2,16,256]{3,2,1,0:T(8,128)S(1)}, u32[]{:S(2)}, u32[]{:S(2)}) collective-permute-start(f32[4,2,16,256]{3,2,1,0:T(8,128)S(1)} %fusion.40), channel_id=1, source_target_pairs={{0,16},{1,17},{2,18},{3,19},{4,20},{5,21},{6,22},{7,23},{8,24},{9,... | collective-permute-start | bytes 393224 | tf_op jit(solution)/shard_map/ppermute | solution.py:31
  68.3 5.6 %all-to-all-start.1 = ((f32[16,1,256]{2,1,0:T(1,128)}), f32[16,1,256]{2,1,0:T(1,128)S(1)}, u32[]{:S(2)}, u32[]{:S(2)}) async-start(f32[16,1,256]{2,1,0:T(1,128)} %reshape.293), calls=%async_computation.1 | async-start | bytes 32768 | tf_op jit(solution)/shard_map/all_to_all | solution.py:139
  74.2 6.1 %all-to-all-done.1 = f32[16,1,256]{2,1,0:T(1,128)S(1)} async-done(((f32[16,1,256]{2,1,0:T(1,128)}), f32[16,1,256]{2,1,0:T(1,128)S(1)}, u32[]{:S(2)}, u32[]{:S(2)}) %all-to-all-start.1) | async-done | bytes 16416 | tf_op jit(solution)/shard_map/all_to_all | solution.py:139
  82.6 6.4 %scatter_custom_fusion.3 = f32[8,4096]{0,1:T(8,128)} fusion(s32[512]{0:T(512)S(1)} %reshape.240, f32[]{:T(128)} %constant.35.clone.1, f32[8,512]{0,1:T(8,128)S(1)} %bitcast.268, f32[]{:T(128)} %constant.83.clone.1, f32[512]{0:T(512)S(1)} %add.188, pred[512]{0:T(512)(128)(4,1)S(1)} %le.21, pred[512]{0:T(512)(128)(4,1)S(1)} %ge.31, f32[8,4096]{0,1:T(8,128)S(1)} %copy.49, ...), kind=kCustom, calls=%fused_computation.46 | custom fusion | flops 20480 | bytes 2499072 | tf_op jit(solution)/shard_map/scatter-add | solution.py:155
  89.0 2.2 %copy.50 = f32[8,4096]{1,0:T(8,128)S(1)} copy(f32[8,4096]{0,1:T(8,128)} %scatter_custom_fusion.3) | data formatting | bytes 262144 | tf_op jit(solution)/shard_map/scatter-add | solution.py:155
  91.3 0.7 multiply_add_fusion
  (108 shorter events, 23.8 us)
Async XLA Ops:
  0.0 29.6 %copy-start.5 = (bf16[3,64,48]{1,2,0:T(8,128)(2,1)S(1)}, bf16[3,64,48]{1,2,0:T(8,128)(2,1)}, u32[]{:S(2)}) copy-start(bf16[3,64,48]{1,2,0:T(8,128)(2,1)} %param.21) | copy-start | bytes 55300
  1.7 20.9 %collective-permute-start = (bf16[4,2,16,256]{3,2,1,0:T(8,128)(2,1)S(1)}, bf16[4,2,16,256]{3,2,1,0:T(8,128)(2,1)S(1)}, u32[]{:S(2)}, u32[]{:S(2)}) collective-permute-start(bf16[4,2,16,256]{3,2,1,0:T(8,128)(2,1)S(1)} %divide_convert_fusion), channel_id=1, source_target_pairs={{16,0},{17,1},{18,2},{19,3},{20,4},{21,5},{22,6},{23,7},{24,8},{25... | collective-permute-start | bytes 196616 | tf_op jit(solution)/shard_map/ppermute | solution.py:31
  15.2 32.3 %all-to-all-start = ((s32[16,1,32]{2,1,0:T(1,128)}), s32[16,1,32]{2,1,0:T(1,128)S(1)}, u32[]{:S(2)}, u32[]{:S(2)}) async-start(s32[16,1,32]{2,1,0:T(1,128)} %constant_dynamic-update-slice_fusion.3), calls=%async_computation | async-start | bytes 16384 | tf_op jit(solution)/shard_map/all_to_all | solution.py:142
  22.7 5.8 %collective-permute-start.1 = (bf16[1,16,1,256]{3,1,2,0:T(8,128)(2,1)S(1)}, bf16[1,16,1,256]{3,1,2,0:T(8,128)(2,1)S(1)}, u32[]{:S(2)}, u32[]{:S(2)}) collective-permute-start(bf16[1,16,1,256]{3,1,2,0:T(8,128)(2,1)S(1)} %copy.56), channel_id=1, source_target_pairs={{0,1},{1,2},{2,3},{3,4},{4,5},{5,6},{6,7},{7,8},{8,9},{9,10},{10,1... | collective-permute-start | bytes 24584 | tf_op jit(solution)/shard_map/ppermute | solution.py:19
  23.9 5.4 %collective-permute-start.2 = (bf16[1,16,1,256]{3,1,2,0:T(8,128)(2,1)S(1)}, bf16[1,16,1,256]{3,1,2,0:T(8,128)(2,1)S(1)}, u32[]{:S(2)}, u32[]{:S(2)}) collective-permute-start(bf16[1,16,1,256]{3,1,2,0:T(8,128)(2,1)S(1)} %copy.57), channel_id=1, source_target_pairs={{1,0},{2,1},{3,2},{4,3},{5,4},{6,5},{7,6},{8,7},{9,8},{10,9},{11,1... | collective-permute-start | bytes 24584 | tf_op jit(solution)/shard_map/ppermute | solution.py:21
  30.3 6.9 %copy-start.6 = (f32[4,2,128]{2,1,0:T(2,128)S(1)}, f32[4,2,128]{2,1,0:T(2,128)}, u32[]{:S(2)}) copy-start(f32[4,2,128]{2,1,0:T(2,128)} %param.17) | copy-start | bytes 12292
  30.9 8.3 %collective-permute-start.3 = (bf16[1,64,1,256]{3,1,2,0:T(8,128)(2,1)S(1)}, bf16[1,64,1,256]{3,1,2,0:T(8,128)(2,1)S(1)}, u32[]{:S(2)}, u32[]{:S(2)}) collective-permute-start(bf16[1,64,1,256]{3,1,2,0:T(8,128)(2,1)S(1)} %get-tuple-element.23), channel_id=1, source_target_pairs={{0,1},{1,2},{2,3},{3,4},{4,5},{5,6},{6,7},{7,8},{8,9},{9,10},{10,1... | collective-permute-start | bytes 98312 | tf_op jit(solution)/shard_map/ppermute | solution.py:19
  30.9 8.2 %collective-permute-start.4 = (bf16[1,64,1,256]{3,1,2,0:T(8,128)(2,1)S(1)}, bf16[1,64,1,256]{3,1,2,0:T(8,128)(2,1)S(1)}, u32[]{:S(2)}, u32[]{:S(2)}) collective-permute-start(bf16[1,64,1,256]{3,1,2,0:T(8,128)(2,1)S(1)} %get-tuple-element.24), channel_id=1, source_target_pairs={{1,0},{2,1},{3,2},{4,3},{5,4},{6,5},{7,6},{8,7},{9,8},{10,9},{11,1... | collective-permute-start | bytes 98312 | tf_op jit(solution)/shard_map/ppermute | solution.py:21
  39.7 1.4 %copy-start.2 = (bf16[3,64,192]{2,1,0:T(8,128)(2,1)S(1)}, bf16[3,64,192]{2,1,0:T(8,128)(2,1)}, u32[]{:S(2)}) copy-start(bf16[3,64,192]{2,1,0:T(8,128)(2,1)} %param.22) | copy-start | bytes 221188
  41.9 0.7 copy-start.7
  43.0 8.0 %collective-permute-start.5 = (bf16[1,64,1,256]{3,1,2,0:T(8,128)(2,1)S(1)}, bf16[1,64,1,256]{3,1,2,0:T(8,128)(2,1)S(1)}, u32[]{:S(2)}, u32[]{:S(2)}) collective-permute-start(bf16[1,64,1,256]{3,1,2,0:T(8,128)(2,1)S(1)} %get-tuple-element.21), channel_id=1, source_target_pairs={{0,1},{1,2},{2,3},{3,4},{4,5},{5,6},{6,7},{7,8},{8,9},{9,10},{10,1... | collective-permute-start | bytes 98312 | tf_op jit(solution)/shard_map/ppermute | solution.py:19
  43.1 8.0 %collective-permute-start.6 = (bf16[1,64,1,256]{3,1,2,0:T(8,128)(2,1)S(1)}, bf16[1,64,1,256]{3,1,2,0:T(8,128)(2,1)S(1)}, u32[]{:S(2)}, u32[]{:S(2)}) collective-permute-start(bf16[1,64,1,256]{3,1,2,0:T(8,128)(2,1)S(1)} %get-tuple-element.22), channel_id=1, source_target_pairs={{1,0},{2,1},{3,2},{4,3},{5,4},{6,5},{7,6},{8,7},{9,8},{10,9},{11,1... | collective-permute-start | bytes 98312 | tf_op jit(solution)/shard_map/ppermute | solution.py:21
  47.5 20.7 %all-to-all-start.2 = ((f32[1,16,32]{2,0,1:T(1,128)}), f32[1,16,32]{2,0,1:T(1,128)S(1)}, u32[]{:S(2)}, u32[]{:S(2)}) async-start(f32[1,16,32]{2,0,1:T(1,128)} %all_to_all.21), calls=%async_computation.2 | async-start | bytes 16384 | tf_op jit(solution)/shard_map/all_to_all | solution.py:140
  51.7 1.4 %copy-start.3 = (bf16[3,64,192]{2,1,0:T(8,128)(2,1)S(1)}, bf16[3,64,192]{2,1,0:T(8,128)(2,1)}, u32[]{:S(2)}) copy-start(bf16[3,64,192]{2,1,0:T(8,128)(2,1)} %param.23) | copy-start | bytes 221188
  54.5 6.1 %collective-permute-start.7 = (bf16[1,64,1,256]{3,1,2,0:T(8,128)(2,1)S(1)}, bf16[1,64,1,256]{3,1,2,0:T(8,128)(2,1)S(1)}, u32[]{:S(2)}, u32[]{:S(2)}) collective-permute-start(bf16[1,64,1,256]{3,1,2,0:T(8,128)(2,1)S(1)} %get-tuple-element.19), channel_id=1, source_target_pairs={{0,1},{1,2},{2,3},{3,4},{4,5},{5,6},{6,7},{7,8},{8,9},{9,10},{10,1... | collective-permute-start | bytes 98312 | tf_op jit(solution)/shard_map/ppermute | solution.py:19
  54.8 5.8 %collective-permute-start.8 = (bf16[1,64,1,256]{3,1,2,0:T(8,128)(2,1)S(1)}, bf16[1,64,1,256]{3,1,2,0:T(8,128)(2,1)S(1)}, u32[]{:S(2)}, u32[]{:S(2)}) collective-permute-start(bf16[1,64,1,256]{3,1,2,0:T(8,128)(2,1)S(1)} %get-tuple-element.20), channel_id=1, source_target_pairs={{1,0},{2,1},{3,2},{4,3},{5,4},{6,5},{7,6},{8,7},{9,8},{10,9},{11,1... | collective-permute-start | bytes 98312 | tf_op jit(solution)/shard_map/ppermute | solution.py:21
  61.1 1.4 %copy-start.4 = (bf16[3,16,192]{2,1,0:T(8,128)(2,1)S(1)}, bf16[3,16,192]{2,1,0:T(8,128)(2,1)}, u32[]{:S(2)}) copy-start(bf16[3,16,192]{2,1,0:T(8,128)(2,1)} %param.24) | copy-start | bytes 55300
  63.2 18.6 %copy-start = (f32[4,2,16,256]{3,2,1,0:T(8,128)S(1)}, f32[4,2,16,256]{3,2,1,0:T(8,128)}, u32[]{:S(2)}) copy-start(f32[4,2,16,256]{3,2,1,0:T(8,128)} %param.14) | copy-start | bytes 393220
  63.7 18.0 %collective-permute-start.9 = (f32[4,2,16,256]{3,2,1,0:T(8,128)S(1)}, f32[4,2,16,256]{3,2,1,0:T(8,128)S(1)}, u32[]{:S(2)}, u32[]{:S(2)}) collective-permute-start(f32[4,2,16,256]{3,2,1,0:T(8,128)S(1)} %fusion.40), channel_id=1, source_target_pairs={{0,16},{1,17},{2,18},{3,19},{4,20},{5,21},{6,22},{7,23},{8,24},{9,... | collective-permute-start | bytes 393224 | tf_op jit(solution)/shard_map/ppermute | solution.py:31
  68.3 12.1 %all-to-all-start.1 = ((f32[16,1,256]{2,1,0:T(1,128)}), f32[16,1,256]{2,1,0:T(1,128)S(1)}, u32[]{:S(2)}, u32[]{:S(2)}) async-start(f32[16,1,256]{2,1,0:T(1,128)} %reshape.293), calls=%async_computation.1 | async-start | bytes 32768 | tf_op jit(solution)/shard_map/all_to_all | solution.py:139
  89.0 2.3 %copy-start.1 = (f32[4,2,16,256]{3,2,1,0:T(8,128)S(1)}, f32[4,2,16,256]{3,2,1,0:T(8,128)}, u32[]{:S(2)}) copy-start(f32[4,2,16,256]{3,2,1,0:T(8,128)} %param.15) | copy-start | bytes 393220
